TPU v7x, 32 devices: a whole 2x2x4 slice. The times are simulated.
32 devices in a mesh: dp: 8 (over z, core), tensor: 4 (over y, x).
Axes of the slice: x: 2, y: 2, z: 4, core: 2. Of those that a mesh axis runs over, the one named last changes fastest.
Arguments:
- tokens: bfloat16 [8192, 1024], P('dp'), may hold values from -6 to 6
- segment_ids: int32 [8, 1024], P('dp'), may hold values from 0 to 7, never falling along the last dimension, each value on 1 to 512 neighbouring positions
- ln1_gain: float32 [1024], replicated, may hold values from 0.1 to 1.9
- ln1_shift: float32 [1024], replicated, may hold values from -1.75 to 1.75
- w_qkv: bfloat16 [3, 1024, 1024], P(None, None, 'tensor'), may hold values from -2 to 2
- b_qv: float32 [2, 1024], P(None, 'tensor'), may hold values from -3 to 3
- w_out: bfloat16 [1024, 1024], P('tensor'), may hold values from -0.75 to 0.75
- b_out: float32 [1024], replicated, may hold values from -3 to 3
- ln2_gain: float32 [1024], replicated, may hold values from 0.1 to 1.9
- ln2_shift: float32 [1024], replicated, may hold values from -1.75 to 1.75
- w_up: bfloat16 [1024, 4096], P(None, 'tensor'), may hold values from -0.1875 to 0.1875
- b_up: float32 [4096], P('tensor'), may hold values from -3 to 3
- w_down: bfloat16 [4096, 1024], P('tensor'), may hold values from -0.09375 to 0.09375
- b_down: float32 [1024], replicated, may hold values from -3 to 3
- d_out: bfloat16 [8192, 1024], P('dp'), may hold values from -6 to 6
Outputs:
- output: bfloat16 [8192, 1024], P('dp')
- d_tokens: bfloat16 [8192, 1024], P('dp')
- g_ln1_gain: float32 [1024], replicated
- g_ln1_shift: float32 [1024], replicated
- g_qkv: float32 [3, 1024, 1024], P(None, None, 'tensor')
- g_qv_bias: float32 [2, 1024], P(None, 'tensor')
- g_out: float32 [1024, 1024], P('tensor')
- g_out_bias: float32 [1024], replicated
- g_ln2_gain: float32 [1024], replicated
- g_ln2_shift: float32 [1024], replicated
- g_up: float32 [1024, 4096], P(None, 'tensor')
- g_up_bias: float32 [4096], P('tensor')
- g_down: float32 [4096, 1024], P('tensor')
- g_down_bias: float32 [1024], replicated
Inputs may be any that keep to these rules, and one draw needn't show every extreme that they name: `segment_ids`: each row numbers its packed sequences from 0 without falling; every sequence has 1 to 512 tokens and one has exactly 512.
All inputs are finite; a program needn't handle non-finite values.
Results may differ from a plain program's by a relative error of at most 0.019.
Values may be sent and summed in bfloat16 or wider, within the bound.
A program may use at most 192 MiB of HBM per device.

v0:
```python
import jax
import jax.numpy as jnp
from jax import lax
from jax.sharding import PartitionSpec as P

HD = 64
epsilon = 1e-05
gelu_coef = 0.7978845608028654


def gelu_value(values):
    inner = jnp.tanh(gelu_coef * (values + 0.044715 * values * values * values))
    return 0.5 * values * (1.0 + inner)


def gelu_slope(values):
    inner = jnp.tanh(gelu_coef * (values + 0.044715 * values * values * values))
    return 0.5 * (1.0 + inner) + 0.5 * values * (1.0 - inner * inner) * gelu_coef * (
        1.0 + 3.0 * 0.044715 * values * values
    )


def norm_parts(values):
    centered = values - jnp.mean(values, axis=-1, keepdims=True)
    inverse = lax.rsqrt(jnp.mean(centered * centered, axis=-1, keepdims=True) + epsilon)
    return (centered * inverse, inverse)


def norm_back(grad_in, normed, inverse, gain):
    scaled = grad_in * gain
    return inverse * (
        scaled
        - jnp.mean(scaled, axis=-1, keepdims=True)
        - normed * jnp.mean(scaled * normed, axis=-1, keepdims=True)
    )


def row_slice(values):
    row_count = values.shape[0] // lax.axis_size("tensor")
    return lax.dynamic_slice_in_dim(values, lax.axis_index("tensor") * row_count, row_count, 0)


def block_mask(seg_query, seg_keys, first_row):
    shape_here = (seg_query.shape[0], seg_keys.shape[0])
    query_pos = first_row + lax.broadcasted_iota(jnp.int32, shape_here, 0)
    key_pos = lax.broadcasted_iota(jnp.int32, shape_here, 1)
    return (seg_query[:, None] == seg_keys[None, :]) & (key_pos <= query_pos)


def attention_forward(query_heads, key_heads, value_heads, seg_row):
    length = query_heads.shape[1]
    block_rows = 512
    scale = query_heads.shape[2] ** (-0.5)
    outputs = []
    totals = []
    for first_row in range(0, length, block_rows):
        rows_q = query_heads[:, first_row : first_row + block_rows]
        scores = (
            jnp.einsum("hqd,hkd->hqk", rows_q, key_heads, preferred_element_type=jnp.float32)
            * scale
        )
        allowed = block_mask(seg_row[first_row : first_row + block_rows], seg_row, first_row)
        scores = jnp.where(allowed[None], scores, -jnp.inf)
        maximum = jnp.max(scores, axis=-1, keepdims=True)
        log_total = jnp.log(jnp.sum(jnp.exp(scores - maximum), axis=-1, keepdims=True)) + maximum
        weights_bf = jnp.exp(scores - log_total).astype(jnp.bfloat16)
        outputs.append(
            jnp.einsum(
                "hqk,hkd->hqd", weights_bf, value_heads, preferred_element_type=jnp.float32
            ).astype(jnp.bfloat16)
        )
        totals.append(log_total)
    return (jnp.concatenate(outputs, axis=1), jnp.concatenate(totals, axis=1))


def attention_backward(query_heads, key_heads, value_heads, seg_row, log_totals, grad_ctx):
    length = query_heads.shape[1]
    block_rows = 512
    scale = query_heads.shape[2] ** (-0.5)
    grad_keys = jnp.zeros(key_heads.shape, jnp.float32)
    grad_values = jnp.zeros(value_heads.shape, jnp.float32)
    grad_queries = []
    for first_row in range(0, length, block_rows):
        rows_q = query_heads[:, first_row : first_row + block_rows]
        scores = (
            jnp.einsum("hqd,hkd->hqk", rows_q, key_heads, preferred_element_type=jnp.float32)
            * scale
        )
        allowed = block_mask(seg_row[first_row : first_row + block_rows], seg_row, first_row)
        scores = jnp.where(allowed[None], scores, -jnp.inf)
        weights = jnp.exp(scores - log_totals[:, first_row : first_row + block_rows])
        weights_bf = weights.astype(jnp.bfloat16)
        grad_rows_ctx = grad_ctx[:, first_row : first_row + block_rows]
        grad_weights = jnp.einsum(
            "hqd,hkd->hqk", grad_rows_ctx, value_heads, preferred_element_type=jnp.float32
        )
        inner_sum = jnp.sum(weights * grad_weights, axis=-1, keepdims=True)
        grad_scores = (weights * (grad_weights - inner_sum)).astype(jnp.bfloat16)
        grad_queries.append(
            (
                jnp.einsum(
                    "hqk,hkd->hqd", grad_scores, key_heads, preferred_element_type=jnp.float32
                )
                * scale
            ).astype(jnp.bfloat16)
        )
        grad_keys = (
            grad_keys
            + jnp.einsum("hqk,hqd->hkd", grad_scores, rows_q, preferred_element_type=jnp.float32)
            * scale
        )
        grad_values = grad_values + jnp.einsum(
            "hqk,hqd->hkd", weights_bf, grad_rows_ctx, preferred_element_type=jnp.float32
        )
    return (
        jnp.concatenate(grad_queries, axis=1),
        grad_keys.astype(jnp.bfloat16),
        grad_values.astype(jnp.bfloat16),
    )


def per_device(
    tokens,
    segment_ids,
    ln1_gain,
    ln1_shift,
    w_qkv,
    b_qv,
    w_out,
    b_out,
    ln2_gain,
    ln2_shift,
    w_up,
    b_up,
    w_down,
    b_down,
    d_out,
):
    seg_row = segment_ids[0]
    length = tokens.shape[0]
    local_width = w_qkv.shape[2]
    head_count = local_width // HD
    tokens_f = tokens.astype(jnp.float32)
    normed1, inverse1 = norm_parts(tokens_f)
    input1 = (normed1 * ln1_gain + ln1_shift).astype(jnp.bfloat16)
    projected = jnp.einsum("sd,ide->ise", input1, w_qkv, preferred_element_type=jnp.float32)
    bias_rows = jnp.stack([b_qv[0], jnp.zeros_like(b_qv[0]), b_qv[1]])
    projected = (projected + bias_rows[:, None, :]).astype(jnp.bfloat16)
    split_heads = projected.reshape(3, length, head_count, HD).transpose(0, 2, 1, 3)
    query_heads, key_heads, value_heads = (split_heads[0], split_heads[1], split_heads[2])
    context_heads, log_totals = attention_forward(query_heads, key_heads, value_heads, seg_row)
    context = context_heads.transpose(1, 0, 2).reshape(length, local_width)
    attn_part = jnp.dot(context, w_out, preferred_element_type=jnp.float32)
    attn_sum = lax.psum(attn_part.astype(jnp.bfloat16), "tensor").astype(jnp.float32)
    resid_mid = tokens_f + attn_sum + b_out
    normed2, inverse2 = norm_parts(resid_mid)
    input2 = (normed2 * ln2_gain + ln2_shift).astype(jnp.bfloat16)
    pre_act = jnp.dot(input2, w_up, preferred_element_type=jnp.float32) + b_up
    activated = gelu_value(pre_act).astype(jnp.bfloat16)
    mlp_part = jnp.dot(activated, w_down, preferred_element_type=jnp.float32)
    mlp_sum = lax.psum(mlp_part.astype(jnp.bfloat16), "tensor").astype(jnp.float32)
    output = (resid_mid + mlp_sum + b_down).astype(jnp.bfloat16)
    grad_out = d_out.astype(jnp.float32)
    grad_rows = row_slice(grad_out)
    g_down_bias = jnp.sum(grad_rows, axis=0)
    g_down = jnp.einsum("sf,sd->fd", activated, d_out, preferred_element_type=jnp.float32)
    grad_act = jnp.einsum("sd,fd->sf", d_out, w_down, preferred_element_type=jnp.float32)
    grad_pre = (grad_act * gelu_slope(pre_act)).astype(jnp.bfloat16)
    g_up = jnp.einsum("sd,sf->df", input2, grad_pre, preferred_element_type=jnp.float32)
    g_up_bias = jnp.sum(grad_pre.astype(jnp.float32), axis=0)
    normed_part = jnp.einsum("sf,df->sd", grad_pre, w_up, preferred_element_type=jnp.float32)
    normed_grad = lax.psum(normed_part.astype(jnp.bfloat16), "tensor").astype(jnp.float32)
    resid_grad = grad_out + norm_back(normed_grad, normed2, inverse2, ln2_gain)
    normed_grad_rows = row_slice(normed_grad)
    g_ln2_gain = jnp.sum(normed_grad_rows * row_slice(normed2), axis=0)
    g_ln2_shift = jnp.sum(normed_grad_rows, axis=0)
    g_out_bias = jnp.sum(row_slice(resid_grad), axis=0)
    resid_grad_bf = resid_grad.astype(jnp.bfloat16)
    g_out = jnp.einsum("sk,sd->kd", context, resid_grad_bf, preferred_element_type=jnp.float32)
    grad_context = jnp.einsum(
        "sd,kd->sk", resid_grad_bf, w_out, preferred_element_type=jnp.float32
    ).astype(jnp.bfloat16)
    grad_ctx_heads = grad_context.reshape(length, head_count, HD).transpose(1, 0, 2)
    grad_q, grad_k, grad_v = attention_backward(
        query_heads, key_heads, value_heads, seg_row, log_totals, grad_ctx_heads
    )
    grad_proj = (
        jnp.stack([grad_q, grad_k, grad_v]).transpose(0, 2, 1, 3).reshape(3, length, local_width)
    )
    g_qkv = jnp.einsum("sd,ise->ide", input1, grad_proj, preferred_element_type=jnp.float32)
    g_qv_bias = jnp.stack(
        [
            jnp.sum(grad_proj[0].astype(jnp.float32), axis=0),
            jnp.sum(grad_proj[2].astype(jnp.float32), axis=0),
        ]
    )
    input_part = jnp.einsum("ise,ide->sd", grad_proj, w_qkv, preferred_element_type=jnp.float32)
    input_grad = lax.psum(input_part.astype(jnp.bfloat16), "tensor").astype(jnp.float32)
    d_tokens = (resid_grad + norm_back(input_grad, normed1, inverse1, ln1_gain)).astype(
        jnp.bfloat16
    )
    input_grad_share = row_slice(input_grad)
    normed1_share = row_slice(normed1)
    g_ln1_gain = jnp.sum(input_grad_share * normed1_share, axis=0)
    g_ln1_shift = jnp.sum(input_grad_share, axis=0)
    g_qkv, g_qv_bias, g_out, g_up, g_up_bias, g_down = lax.psum(
        (g_qkv, g_qv_bias, g_out, g_up, g_up_bias, g_down), "dp"
    )
    g_ln1_gain, g_ln1_shift, g_out_bias, g_ln2_gain, g_ln2_shift, g_down_bias = lax.psum(
        (g_ln1_gain, g_ln1_shift, g_out_bias, g_ln2_gain, g_ln2_shift, g_down_bias),
        ("dp", "tensor"),
    )
    return (
        output,
        d_tokens,
        g_ln1_gain,
        g_ln1_shift,
        g_qkv,
        g_qv_bias,
        g_out,
        g_out_bias,
        g_ln2_gain,
        g_ln2_shift,
        g_up,
        g_up_bias,
        g_down,
        g_down_bias,
    )


def solution(mesh):
    placed = (
        P("dp", None),
        P("dp", None),
        P(),
        P(),
        P(None, None, "tensor"),
        P(None, "tensor"),
        P("tensor", None),
        P(),
        P(),
        P(),
        P(None, "tensor"),
        P("tensor"),
        P("tensor", None),
        P(),
        P("dp", None),
    )
    return jax.shard_map(
        per_device,
        mesh=mesh,
        in_specs=placed,
        out_specs=(
            P("dp", None),
            P("dp", None),
            P(),
            P(),
            P(None, None, "tensor"),
            P(None, "tensor"),
            P("tensor", None),
            P(),
            P(),
            P(),
            P(None, "tensor"),
            P("tensor"),
            P("tensor", None),
            P(),
        ),
        check_vma=False,
    )
```

profile of v0, /device:TPU:0, one launch (start us, length us, event | category | flops | bytes accessed | tf_op | source)
XLA Modules:
  0.0 623.6 jit_solution(2085231049071354112)
XLA Ops:
  34.1 72.3 %all-reduce.9.cloned.1.call-done = bf16[1024,1024]{1,0:T(8,128)(2,1)} async-done(((bf16[1024,1024]{1,0:T(8,128)(2,1)}), bf16[1024,1024]{1,0:T(8,128)(2,1)}) %all-reduce.9.cloned.1.call-update) | async-done | bytes 2097168 | tf_op jit(solution)/shard_map/psum | solution.py:154
  115.7 4.9 convert_reduce_fusion.1
  121.9 3.7 convolution_convert_fusion
  125.9 6.3 %convolution_convert_fusion.1 = bf16[1024,1024]{1,0:T(8,128)(2,1)} fusion(bf16[1024,1024]{1,0:T(8,128)(2,1)S(1)} %copy-done, f32[1024,1024]{1,0:T(8,128)} %copy-done.41, f32[1024]{0:T(1024)S(1)} %copy-done.38), kind=kOutput, calls=%fused_computation.53 | convolution fusion | flops 2159017984 | bytes 8392704 | tf_op jit(solution)/shard_map/dot_general | solution.py:160
  132.2 63.1 %all-reduce.11.cloned.1.call-done = bf16[1024,1024]{1,0:T(8,128)(2,1)} async-done(((bf16[1024,1024]{1,0:T(8,128)(2,1)}), bf16[1024,1024]{1,0:T(8,128)(2,1)}) %all-reduce.11.cloned.1.call-update) | async-done | bytes 2097168 | tf_op jit(solution)/shard_map/psum | solution.py:172
  195.3 3.8 multiply_reduce_fusion.6
  199.1 3.7 multiply_add_fusion.1
  205.7 3.3 fusion.37
  212.1 5.4 multiply_reduce_fusion.1
  217.5 9.7 %multiply_convert_fusion = (bf16[4,512,1024]{2,1,0:T(8,128)(2,1)}, bf16[4,512,1024]{2,1,0:T(8,128)(2,1)}) fusion(f32[4,512,1024]{2,1,0:T(8,128)S(1)} %get-tuple-element.70, f32[4,512,1024]{2,1,0:T(8,128)S(1)} %bitcast.76, f32[4,512]{1,0:T(4,128)S(1)} %get-tuple-element.69, f32[4,512]{1,0:T(4,128)S(1)} %log_add_fusion, ...), kind=kLoop, calls=%fused_computation | loop fusion | flops 25165824 | bytes 43024384 | tf_op jit(solution)/shard_map/convert_element_type | solution.py:98
  227.2 3.8 fusion.24
  239.5 3.2 bitcast_convert_fusion
  243.0 7.3 %fusion.29 = f32[1024,1024]{1,0:T(8,128)} fusion(bf16[1024,1024]{1,0:T(8,128)(2,1)} %copy-done.43, f32[1024,1024]{1,0:T(8,128)} %copy-done.9, f32[1024]{0:T(1024)S(1)} %copy-done.37, f32[1024]{0:T(1024)S(1)} %copy-done.32), kind=kOutput, calls=%fused_computation.81 | convolution fusion | flops 2150629376 | bytes 10493952 | tf_op jit(solution)/shard_map/sd,sf->df/dot_general | solution.py:169
  250.3 5.1 fusion.52
  257.8 3.6 convolution_bitcast_fusion
  261.5 4.0 convert_element_type.118
  268.4 4.0 convert_element_type.121
  272.4 17.1 %all-reduce.1 = (f32[2,256]{1,0:T(2,128)}, f32[1024]{0:T(1024)}) all-reduce(f32[2,256]{1,0:T(2,128)S(1)} %pad_maximum_fusion.3, f32[1024]{0:T(1024)S(1)} %get-tuple-element.71), channel_id=1, replica_groups=mesh['dp'=8,'tensor'=4] {'dp'}, use_global_device_ids=true, to_apply=%region_25.26 | all-reduce | flops 1536 | bytes 12288 | tf_op jit(solution)/shard_map/psum | solution.py:206
  292.7 53.8 %all-reduce.15.cloned.1.call-done = (bf16[1024,1024]{1,0:T(8,128)(2,1)}, bf16[1024,1024]{1,0:T(8,128)(2,1)}) async-done(((bf16[1024,1024]{1,0:T(8,128)(2,1)}, bf16[1024,1024]{1,0:T(8,128)(2,1)}), (bf16[1024,1024]{1,0:T(8,128)(2,1)}, bf16[1024,1024]{1,0:T(8,128)(2,1)})) %all-reduce.15.cloned.1.call-update) | async-done | bytes 4194320 | tf_op jit(solution)/shard_map/psum | solution.py:161
  350.7 41.5 %all-reduce = (f32[1024]{0:T(1024)}, f32[1024]{0:T(1024)}, f32[1024]{0:T(1024)}, f32[1024]{0:T(1024)}, f32[1024]{0:T(1024)}, /*index=5*/f32[1024]{0:T(1024)}) all-reduce(f32[1024]{0:T(1024)S(1)} %get-tuple-element.31, f32[1024]{0:T(1024)S(1)} %get-tuple-element.30, ...), channel_id=1, replica_groups=mesh['dp'=8,'tensor'=4] {'dp','tensor'}, use_global_device_ids=true, to_apply=%region_19.20 | all-reduce | flops 6144 | bytes 49152 | tf_op jit(solution)/shard_map/psum | solution.py:209
  392.2 6.7 %add_convert_fusion = (bf16[1024,1024]{1,0:T(8,128)(2,1)}, bf16[1024,1024]{1,0:T(8,128)(2,1)}) fusion(f32[1024,1024]{1,0:T(8,128)} %copy-done.5, bf16[1024,1024]{1,0:T(8,128)(2,1)} %get-tuple-element.51, f32[1024]{0:T(1024)S(1)} %broadcast_multiply_fusion, f32[1024]{0:T(1024)S(1)} %broadcast_multiply_fusion.1, f32[1024]{0:T(1024)S(1)} %copy-done.30, ...), kind=kLoop, calls=%fused_computation.32 | loop fusion | flops 18874368 | bytes 16805888 | tf_op jit(solution)/shard_map/convert_element_type | solution.py:199
  398.8 206.4 %all-reduce.13.cloned.1.call-done = (f32[3,1024,256]{1,2,0:T(8,128)}, f32[256,1024]{1,0:T(8,128)}, f32[1024,1024]{1,0:T(8,128)}, f32[1024,1024]{1,0:T(8,128)}) async-done(((f32[3,1024,256]{1,2,0:T(8,128)}, f32[256,1024]{1,0:T(8,128)}, f32[1024,1024]{1,0:T(8,128)}, f32[1024,1024]{1,0:T(8,128)}), (f32[3,1024,256]{1,2,0:T(8,128)}, f32[256,1024]{1,0:T(8,128)}, f32[1024,1024]{1,0:T(8,128)}, ...) | async-done | bytes 12582928 | tf_op jit(solution)/shard_map/psum | solution.py:206
  605.3 3.6 copy.31
  609.9 4.9 copy.43
  (159 shorter events, 67.9 us)
Async XLA Ops:
  7.2 107.8 %copy-start = (bf16[1024,1024]{1,0:T(8,128)(2,1)S(1)}, bf16[1024,1024]{1,0:T(8,128)(2,1)}, u32[]{:S(2)}) copy-start(bf16[1024,1024]{1,0:T(8,128)(2,1)} %param.27) | copy-start | bytes 6291460
  7.2 5.6 copy-start.31
  7.2 5.7 copy-start.30
  7.2 5.7 copy-start.39
  7.2 99.2 %all-reduce.9.cloned.1.call-start = ((), (), s32[]{:S(2)}) async-start(), calls=%async_computation | async-start | bytes 4194304 | tf_op jit(solution)/shard_map/psum | solution.py:154
  7.3 5.7 copy-start.2
  7.3 5.7 copy-start.35
  15.6 12.6 %copy-start.24 = (bf16[1024,3,256]{0,2,1:T(8,128)(2,1)}, bf16[1024,3,256]{0,2,1:T(8,128)(2,1)S(1)}, u32[]{:S(2)}) copy-start(bf16[1024,3,256]{0,2,1:T(8,128)(2,1)S(1)} %add_convert_fusion.4) | copy-start | bytes 4718596
  15.7 8.3 %copy-start.20 = (bf16[4,1024,64]{1,2,0:T(8,128)(2,1)}, bf16[4,1024,64]{1,2,0:T(8,128)(2,1)S(1)}, u32[]{:S(2)}) copy-start(bf16[4,1024,64]{1,2,0:T(8,128)(2,1)S(1)} %slice_bitcast_fusion.2) | copy-start | bytes 1572868
  31.1 75.3 %copy-start.29 = (f32[1024]{0:T(1024)S(1)}, f32[1024]{0:T(1024)}, u32[]{:S(2)}) copy-start(f32[1024]{0:T(1024)} %param.22) | copy-start | bytes 12292
  34.1 161.2 %all-reduce.11.cloned.1.call-start = ((), (), s32[]{:S(2)}) async-start(), calls=%async_computation.1 | async-start | bytes 4194304 | tf_op jit(solution)/shard_map/psum | solution.py:172
  115.7 4.9 copy-start.41
  125.6 220.9 %all-reduce.15.cloned.1.call-start = ((), (), s32[]{:S(2)}) async-start(), calls=%async_computation.3 | async-start | bytes 8388608 | tf_op jit(solution)/shard_map/psum | solution.py:161
  195.2 10.4 %slice-start.2 = ((s8[8388608]{0:T(1024)(128)(4,1)}), s8[4194304]{0:T(1024)(128)(4,1)S(1)}, s32[]{:S(2)}) async-start(s8[8388608]{0:T(1024)(128)(4,1)} %bitcast.77), calls=%async_computation.6 | async-start | bytes 8388608
  199.1 5.7 copy-start.23
  199.1 6.5 %slice-start.3 = ((s8[8388608]{0:T(1024)(128)(4,1)}), s8[4194304]{0:T(1024)(128)(4,1)S(1)}, s32[]{:S(2)}) async-start(s8[8388608]{0:T(1024)(128)(4,1)} %bitcast.77), calls=%async_computation.7 | async-start | bytes 8388608
  242.7 7.6 %copy-start.16 = (bf16[1024,1024]{1,0:T(8,128)(2,1)S(1)}, bf16[1024,1024]{1,0:T(8,128)(2,1)}, u32[]{:S(2)}) copy-start(bf16[1024,1024]{1,0:T(8,128)(2,1)} %param.29) | copy-start | bytes 6291460
  242.7 362.5 %all-reduce.13.cloned.1.call-start = ((), (), s32[]{:S(2)}) async-start(), calls=%async_computation.2 | async-start | bytes 25165824 | tf_op jit(solution)/shard_map/psum | solution.py:206
  243.0 7.3 %copy-start.42 = (f32[1024,1024]{1,0:T(8,128)S(1)}, f32[1024,1024]{1,0:T(8,128)}, u32[]{:S(2)}) copy-start(f32[1024,1024]{1,0:T(8,128)} %copy-done.41) | copy-start | bytes 12582916
  250.3 5.1 copy-start.6
  250.3 5.1 copy-start.18
  348.7 43.5 %copy-start.33 = (f32[1024]{0:T(1024)S(1)}, f32[1024]{0:T(1024)}, u32[]{:S(2)}) copy-start(f32[1024]{0:T(1024)} %param.28) | copy-start | bytes 12292
  609.9 4.9 copy-start.19
  609.9 7.0 %copy-start.1 = (bf16[1024,1024]{1,0:T(8,128)(2,1)S(1)}, bf16[1024,1024]{1,0:T(8,128)(2,1)}, u32[]{:S(2)}) copy-start(bf16[1024,1024]{1,0:T(8,128)(2,1)} %param.27) | copy-start | bytes 6291460
  (28 other events, 72.7 us)
Sparse Core Ops, SparseCore 0:
  34.2 72.1 all-reduce.8
  125.7 69.4 all-reduce.10
  242.8 103.6 all-reduce.14
  349.5 255.6 all-reduce.12
where the time goes:
time: 632 us; the launch traced here: 624 us
  waiting for transfers between devices  396 us (63%)
  matrix products  72.4 us (11%)
  other arithmetic  59.1 us (9%)
  blocking collectives  58.6 us (9%)
  local copies, waits for them, and re-layouts  22.6 us (4%)
  between operations  14.6 us (2%)
    psum x1, waiting for transfers between devices, per_device(): lax.psum((g_qkv, g_qv_bias, g_out, g_up, g_up_bias, g_down), 'dp')  206 us
    psum x1, waiting for transfers between devices, per_device(): lax.psum(attn_part.astype(jnp.bfloat16), 'tensor').astype(jnp.float32)  72.3 us
    psum x1, waiting for transfers between devices, per_device(): lax.psum(normed_part.astype(jnp.bfloat16), 'tensor').astype(jnp.float32)  63.1 us
    psum x1, waiting for transfers between devices, per_device(): lax.psum(mlp_part.astype(jnp.bfloat16), 'tensor').astype(jnp.float32)  53.8 us
    psum x1, blocking collectives, per_device(): lax.psum((g_ln1_gain, g_ln1_shift, g_out_bias, g_ln2_gain, g_ln2_shift, g...  41.5 us
    unnamed x100, local copies, waits for them, and re-layouts  21.5 us
    psum x1, blocking collectives, per_device(): lax.psum((g_qkv, g_qv_bias, g_out, g_up, g_up_bias, g_down), 'dp')  17.1 us
  transfers between devices with their start and end apart: 4, of which 4 were waited for; matrix products, arithmetic and copies ran while one was open for 8% of the time, Pallas kernels for 0%

commit v1 on v0

--- a/solution.py
+++ b/solution.py
@@ -151,7 +151,9 @@
     context_heads, log_totals = attention_forward(query_heads, key_heads, value_heads, seg_row)
     context = context_heads.transpose(1, 0, 2).reshape(length, local_width)
     attn_part = jnp.dot(context, w_out, preferred_element_type=jnp.float32)
-    attn_sum = lax.psum(attn_part.astype(jnp.bfloat16), "tensor").astype(jnp.float32)
+    attn_sum = jnp.sum(lax.all_gather(attn_part.astype(jnp.bfloat16), "tensor"), axis=0).astype(
+        jnp.float32
+    )
     resid_mid = tokens_f + attn_sum + b_out
     normed2, inverse2 = norm_parts(resid_mid)
     input2 = (normed2 * ln2_gain + ln2_shift).astype(jnp.bfloat16)

time: 632 us -> 658 us (1.041)
  waiting for transfers between devices: 396 us -> 414 us
  other arithmetic: 59.1 us -> 66.6 us
    all_gather x0 -> x1, waiting for transfers between devices: none -> 90.3 us  [per_device(): lax.all_gather(attn_part.astype(jnp.bfloat16), 'tensor')]
    psum x1 -> x0, waiting for transfers between devices: 72.3 us -> none  [per_device(): lax.psum(attn_part.astype(jnp.bfloat16), 'tensor').astype(jnp.float32)]
    reduce_sum x0 -> x1, other arithmetic: none -> 7.44 us  [per_device(): jnp.sum(lax.all_gather(attn_part.astype(jnp.bfloat16), 'tensor'), axis=0)]
where the time goes in v1:
time: 658 us; the launch traced here: 650 us
  waiting for transfers between devices  414 us (63%)
  matrix products  72.9 us (11%)
  other arithmetic  66.6 us (10%)
  blocking collectives  58.7 us (9%)
  local copies, waits for them, and re-layouts  22.6 us (3%)
  between operations  14.9 us (2%)
    psum x1, waiting for transfers between devices, per_device(): lax.psum((g_qkv, g_qv_bias, g_out, g_up, g_up_bias, g_down), 'dp')  206 us
    all_gather x1, waiting for transfers between devices, per_device(): lax.all_gather(attn_part.astype(jnp.bfloat16), 'tensor')  90.3 us
    psum x1, waiting for transfers between devices, per_device(): lax.psum(normed_part.astype(jnp.bfloat16), 'tensor').astype(jnp.float32)  63.2 us
    psum x1, waiting for transfers between devices, per_device(): lax.psum(mlp_part.astype(jnp.bfloat16), 'tensor').astype(jnp.float32)  53.8 us
    psum x1, blocking collectives, per_device(): lax.psum((g_ln1_gain, g_ln1_shift, g_out_bias, g_ln2_gain, g_ln2_shift, g...  41.5 us
    unnamed x100, local copies, waits for them, and re-layouts  21.4 us
    psum x1, blocking collectives, per_device(): lax.psum((g_qkv, g_qv_bias, g_out, g_up, g_up_bias, g_down), 'dp')  17.1 us
  transfers between devices with their start and end apart: 4, of which 4 were waited for; matrix products, arithmetic and copies ran while one was open for 8% of the time, Pallas kernels for 0%

profile of v1, /device:TPU:0, one launch (start us, length us, event | category | flops | bytes accessed | tf_op | source)
XLA Modules:
  0.0 649.7 jit_solution(14629066574958607265)
XLA Ops:
  34.1 90.3 %all-gather.3.cloned.1.call-done = bf16[4096,1024]{1,0:T(8,128)(2,1)} async-done(((bf16[1024,1024]{1,0:T(8,128)(2,1)}), bf16[4096,1024]{1,0:T(8,128)(2,1)}) %all-gather.3.cloned.1.call-update) | async-done | bytes 8388624 | tf_op jit(solution)/shard_map/all_gather | solution.py:154
  124.4 7.4 %reduce_sum.205 = bf16[1024,1024]{1,0:T(8,128)(2,1)} reduce(bf16[4,1024,1024]{2,1,0:T(8,128)(2,1)} %bitcast.80, bf16[]{:T(256)} %constant.13.clone.1), dimensions={0}, to_apply=%region_6.7 | reduce | flops 3145728 | bytes 10485762 | tf_op jit(solution)/shard_map/reduce_sum | solution.py:154
  141.1 5.3 convert_reduce_fusion.1
  147.7 3.7 convolution_convert_fusion
  151.5 6.4 convolution_convert_fusion.1
  157.9 63.2 %all-reduce.8.cloned.1.call-done = bf16[1024,1024]{1,0:T(8,128)(2,1)} async-done(((bf16[1024,1024]{1,0:T(8,128)(2,1)}), bf16[1024,1024]{1,0:T(8,128)(2,1)}) %all-reduce.8.cloned.1.call-update) | async-done | bytes 2097168 | tf_op jit(solution)/shard_map/psum | solution.py:174
  221.1 3.8 multiply_reduce_fusion.6
  225.0 3.9 multiply_add_fusion.1
  231.7 3.3 fusion.37
  238.1 5.4 multiply_reduce_fusion.1
  243.5 9.5 %multiply_convert_fusion = (bf16[4,512,1024]{2,1,0:T(8,128)(2,1)}, bf16[4,512,1024]{2,1,0:T(8,128)(2,1)}) fusion(f32[4,512,1024]{2,1,0:T(8,128)S(1)} %get-tuple-element.70, f32[4,512,1024]{2,1,0:T(8,128)S(1)} %bitcast.77, f32[4,512]{1,0:T(4,128)S(1)} %get-tuple-element.69, f32[4,512]{1,0:T(4,128)S(1)} %log_add_fusion, ...), kind=kLoop, calls=%fused_computation | loop fusion | flops 25165824 | bytes 43024384 | tf_op jit(solution)/shard_map/convert_element_type | solution.py:98
  253.0 3.8 fusion.24
  268.9 7.3 %fusion.29 = f32[1024,1024]{1,0:T(8,128)} fusion(bf16[1024,1024]{1,0:T(8,128)(2,1)} %copy-done.43, f32[1024,1024]{1,0:T(8,128)} %copy-done.10, f32[1024]{0:T(1024)S(1)} %copy-done.37, f32[1024]{0:T(1024)S(1)} %copy-done.32), kind=kOutput, calls=%fused_computation.81 | convolution fusion | flops 2150629376 | bytes 10493952 | tf_op jit(solution)/shard_map/sd,sf->df/dot_general | solution.py:171
  276.2 5.1 fusion.52
  283.7 3.6 convolution_bitcast_fusion
  287.4 4.0 convert_element_type.120
  294.3 4.0 convert_element_type.123
  298.3 17.1 %all-reduce.1 = (f32[2,256]{1,0:T(2,128)}, f32[1024]{0:T(1024)}) all-reduce(f32[2,256]{1,0:T(2,128)S(1)} %pad_maximum_fusion.3, f32[1024]{0:T(1024)S(1)} %get-tuple-element.71), channel_id=1, replica_groups=mesh['dp'=8,'tensor'=4] {'dp'}, use_global_device_ids=true, to_apply=%region_25.26 | all-reduce | flops 1536 | bytes 12288 | tf_op jit(solution)/shard_map/psum | solution.py:208
  318.5 53.8 %all-reduce.12.cloned.1.call-done = (bf16[1024,1024]{1,0:T(8,128)(2,1)}, bf16[1024,1024]{1,0:T(8,128)(2,1)}) async-done(((bf16[1024,1024]{1,0:T(8,128)(2,1)}, bf16[1024,1024]{1,0:T(8,128)(2,1)}), (bf16[1024,1024]{1,0:T(8,128)(2,1)}, bf16[1024,1024]{1,0:T(8,128)(2,1)})) %all-reduce.12.cloned.1.call-update) | async-done | bytes 4194320 | tf_op jit(solution)/shard_map/psum | solution.py:163
  376.5 41.5 %all-reduce = (f32[1024]{0:T(1024)}, f32[1024]{0:T(1024)}, f32[1024]{0:T(1024)}, f32[1024]{0:T(1024)}, f32[1024]{0:T(1024)}, /*index=5*/f32[1024]{0:T(1024)}) all-reduce(f32[1024]{0:T(1024)S(1)} %get-tuple-element.31, f32[1024]{0:T(1024)S(1)} %get-tuple-element.30, ...), channel_id=1, replica_groups=mesh['dp'=8,'tensor'=4] {'dp','tensor'}, use_global_device_ids=true, to_apply=%region_19.20 | all-reduce | flops 6144 | bytes 49152 | tf_op jit(solution)/shard_map/psum | solution.py:211
  418.1 6.7 %add_convert_fusion = (bf16[1024,1024]{1,0:T(8,128)(2,1)}, bf16[1024,1024]{1,0:T(8,128)(2,1)}) fusion(f32[1024,1024]{1,0:T(8,128)} %copy-done.5, bf16[1024,1024]{1,0:T(8,128)(2,1)} %get-tuple-element.51, f32[1024]{0:T(1024)S(1)} %broadcast_multiply_fusion, f32[1024]{0:T(1024)S(1)} %broadcast_multiply_fusion.1, f32[1024]{0:T(1024)S(1)} %copy-done.30, ...), kind=kLoop, calls=%fused_computation.32 | loop fusion | flops 18874368 | bytes 16805888 | tf_op jit(solution)/shard_map/convert_element_type | solution.py:201
  424.8 206.3 %all-reduce.10.cloned.1.call-done = (f32[3,1024,256]{1,2,0:T(8,128)}, f32[256,1024]{1,0:T(8,128)}, f32[1024,1024]{1,0:T(8,128)}, f32[1024,1024]{1,0:T(8,128)}) async-done(((f32[3,1024,256]{1,2,0:T(8,128)}, f32[256,1024]{1,0:T(8,128)}, f32[1024,1024]{1,0:T(8,128)}, f32[1024,1024]{1,0:T(8,128)}), (f32[3,1024,256]{1,2,0:T(8,128)}, f32[256,1024]{1,0:T(8,128)}, f32[1024,1024]{1,0:T(8,128)}, ...) | async-done | bytes 12582928 | tf_op jit(solution)/shard_map/psum | solution.py:208
  631.1 3.6 copy.31
  635.7 4.9 copy.42
  (160 shorter events, 70.9 us)
Async XLA Ops:
  7.2 133.2 %copy-start = (bf16[1024,1024]{1,0:T(8,128)(2,1)S(1)}, bf16[1024,1024]{1,0:T(8,128)(2,1)}, u32[]{:S(2)}) copy-start(bf16[1024,1024]{1,0:T(8,128)(2,1)} %param.27) | copy-start | bytes 6291460
  7.2 5.6 copy-start.31
  7.2 5.7 copy-start.30
  7.2 5.7 copy-start.39
  7.2 117.2 %all-gather.3.cloned.1.call-start = ((), (), s32[]{:S(2)}) async-start(), calls=%async_computation.1 | async-start | bytes 10485760 | tf_op jit(solution)/shard_map/all_gather | solution.py:154
  7.3 5.7 copy-start.2
  7.3 5.7 copy-start.35
  15.6 12.6 %copy-start.24 = (bf16[1024,3,256]{0,2,1:T(8,128)(2,1)}, bf16[1024,3,256]{0,2,1:T(8,128)(2,1)S(1)}, u32[]{:S(2)}) copy-start(bf16[1024,3,256]{0,2,1:T(8,128)(2,1)S(1)} %add_convert_fusion.4) | copy-start | bytes 4718596
  15.7 8.3 %copy-start.20 = (bf16[4,1024,64]{1,2,0:T(8,128)(2,1)}, bf16[4,1024,64]{1,2,0:T(8,128)(2,1)S(1)}, u32[]{:S(2)}) copy-start(bf16[4,1024,64]{1,2,0:T(8,128)(2,1)S(1)} %slice_bitcast_fusion.2) | copy-start | bytes 1572868
  34.1 187.0 %all-reduce.8.cloned.1.call-start = ((), (), s32[]{:S(2)}) async-start(), calls=%async_computation | async-start | bytes 4194304 | tf_op jit(solution)/shard_map/psum | solution.py:174
  124.4 7.4 %copy-start.29 = (f32[1024]{0:T(1024)S(1)}, f32[1024]{0:T(1024)}, u32[]{:S(2)}) copy-start(f32[1024]{0:T(1024)} %param.22) | copy-start | bytes 12292
  141.1 5.3 copy-start.41
  151.5 220.9 %all-reduce.12.cloned.1.call-start = ((), (), s32[]{:S(2)}) async-start(), calls=%async_computation.3 | async-start | bytes 8388608 | tf_op jit(solution)/shard_map/psum | solution.py:163
  221.1 10.5 %slice-start.2 = ((s8[8388608]{0:T(1024)(128)(4,1)}), s8[4194304]{0:T(1024)(128)(4,1)S(1)}, s32[]{:S(2)}) async-start(s8[8388608]{0:T(1024)(128)(4,1)} %bitcast.78), calls=%async_computation.6 | async-start | bytes 8388608
  224.9 5.9 copy-start.23
  225.0 6.7 %slice-start.3 = ((s8[8388608]{0:T(1024)(128)(4,1)}), s8[4194304]{0:T(1024)(128)(4,1)S(1)}, s32[]{:S(2)}) async-start(s8[8388608]{0:T(1024)(128)(4,1)} %bitcast.78), calls=%async_computation.7 | async-start | bytes 8388608
  268.5 7.6 %copy-start.16 = (bf16[1024,1024]{1,0:T(8,128)(2,1)S(1)}, bf16[1024,1024]{1,0:T(8,128)(2,1)}, u32[]{:S(2)}) copy-start(bf16[1024,1024]{1,0:T(8,128)(2,1)} %param.29) | copy-start | bytes 6291460
  268.5 362.6 %all-reduce.10.cloned.1.call-start = ((), (), s32[]{:S(2)}) async-start(), calls=%async_computation.2 | async-start | bytes 25165824 | tf_op jit(solution)/shard_map/psum | solution.py:208
  268.8 7.3 %copy-start.42 = (f32[1024,1024]{1,0:T(8,128)S(1)}, f32[1024,1024]{1,0:T(8,128)}, u32[]{:S(2)}) copy-start(f32[1024,1024]{1,0:T(8,128)} %copy-done.41) | copy-start | bytes 12582916
  276.2 5.1 copy-start.6
  276.2 5.1 copy-start.18
  374.6 43.5 %copy-start.33 = (f32[1024]{0:T(1024)S(1)}, f32[1024]{0:T(1024)}, u32[]{:S(2)}) copy-start(f32[1024]{0:T(1024)} %param.28) | copy-start | bytes 12292
  635.7 4.9 copy-start.19
  635.7 7.0 %copy-start.1 = (bf16[1024,1024]{1,0:T(8,128)(2,1)S(1)}, bf16[1024,1024]{1,0:T(8,128)(2,1)}, u32[]{:S(2)}) copy-start(bf16[1024,1024]{1,0:T(8,128)(2,1)} %param.27) | copy-start | bytes 6291460
  (28 other events, 72.7 us)
Sparse Core Ops, SparseCore 0:
  34.2 90.1 all-gather.2
  151.6 69.4 all-reduce.7
  268.6 103.6 all-reduce.11
  375.4 255.6 all-reduce.9
